TPU v7x, 256 devices: a whole 4x4x8 slice. The times are simulated.
256 devices in a mesh: shard: 32 (over z, y), dp: 8 (over x, core).
Axes of the slice: x: 4, y: 4, z: 8, core: 2. Of those that a mesh axis runs over, the one named last changes fastest.
Arguments:
- cold_table: bfloat16 [65536, 256], P('shard'), may hold values from -6 to 6
- cold_accum: float32 [65536], P('shard'), may hold values from 0.005 to 0.5
- dither_bits: int32 [65536, 256], P('shard'), may hold values from 0 to 65280
- hot_table: float32 [1024, 256], replicated, may hold values from -6 to 6
- hot_accum: float32 [1024], replicated, may hold values from 1 to 100
- w_flat: bfloat16 [4096, 512], replicated, may hold values from -0.09375 to 0.09375
- w_inter: bfloat16 [256, 512], replicated, may hold values from -0.09375 to 0.09375
- hidden_bias: float32 [512], replicated, may hold values from -1 to 1
- w_out: float32 [512], replicated, may hold values from -0.25 to 0.25
- targets: float32 [131072], P(('shard', 'dp')), may hold values from 0 to 1
- hot_ids: int32 [131072, 8], P(('shard', 'dp')), may hold values from 0 to 1023
- cold_slots: int32 [131072, 8], P(('shard', 'dp')), may hold values from 0 to 2047, as said below
- requests: int32 [16384, 64], P(('shard', 'dp')), may hold values from 0 to 2047, as said below
- counts: int32 [512, 32], P(('shard', 'dp')), may hold values from 1 to 64, as said below
Outputs:
- cold_out: bfloat16 [65536, 256], P('shard')
- cold_accum_out: float32 [65536], P('shard')
- hot_out: float32 [1024, 256], replicated
- hot_accum_out: float32 [1024], replicated
Inputs may be any that keep to these rules, and one draw needn't show every extreme that they name: `requests`: in each row of 64 entries (one device, micro-batch and shard) the entries name distinct rows of that shard's 2048; only the first counts-many are live, the rest name arbitrary rows. `counts`: in every draw, each device has in each micro-batch a shard with exactly 64 live slots. `cold_slots`: index into its device's request rows of that micro-batch, shard * 64 + slot; always a live slot, and every live slot is named by some lookup.
All inputs are finite; a program needn't handle non-finite values.
Results may differ from a plain program's by a relative error of at most 0.001.
The roundings to bfloat16 on the way count: a program that leaves them out, or rounds other values in their place, can miss the bound.
Values may be sent and summed in bfloat16 or wider, within the bound.
No kernel may reach another device: no remote copies, remote signals or barrier semaphores. Data moves between devices by JAX's collectives and lax.ppermute only.
A program may use at most 128 MiB of HBM per device.

v0:
```python
import jax
import jax.numpy as jnp
from jax import lax
from jax.sharding import PartitionSpec as P

MB = 2
BATCH = 256
learn_rate = 0.3


def backprop(stacked, targets, w_flat, w_inter, hidden_bias, w_out):
    row_count, feature_count, row_width = stacked.shape
    flattened = stacked.reshape(row_count, feature_count * row_width)
    pair_dots = (
        jnp.einsum("sfe,sge->sfg", stacked, stacked, preferred_element_type=jnp.float32)
        * row_width ** (-0.5)
    ).astype(jnp.bfloat16)
    pre_act = jnp.dot(flattened, w_flat, preferred_element_type=jnp.float32)
    pre_act = pre_act + jnp.dot(
        pair_dots.reshape(row_count, feature_count * feature_count),
        w_inter,
        preferred_element_type=jnp.float32,
    )
    pre_act = pre_act + hidden_bias
    gated = jax.nn.sigmoid(pre_act)
    logits = jnp.sum(pre_act * gated * w_out, axis=-1)
    residual = jax.nn.sigmoid(logits) - targets
    slopes = (residual[:, None] * w_out * gated * (1.0 + pre_act * (1.0 - gated))).astype(
        jnp.bfloat16
    )
    back_flat = jnp.dot(slopes, w_flat.T, preferred_element_type=jnp.float32)
    back_pairs = jnp.dot(slopes, w_inter.T, preferred_element_type=jnp.float32).reshape(
        row_count, feature_count, feature_count
    )
    mirror = ((back_pairs + jnp.swapaxes(back_pairs, 1, 2)) * row_width ** (-0.5)).astype(
        jnp.bfloat16
    )
    return back_flat.reshape(row_count, feature_count, row_width) + jnp.einsum(
        "sfg,sge->sfe", mirror, stacked, preferred_element_type=jnp.float32
    )


def adagrad_rows(table_rows, accum, gradient):
    accum_new = accum + jnp.mean(gradient * gradient, axis=-1)
    updated = table_rows - learn_rate * gradient / jnp.sqrt(accum_new)[:, None]
    return (updated, accum_new)


def requantize(updated, bits, touched):
    grid_step = jnp.max(jnp.abs(updated), axis=-1, keepdims=True) / 8.0
    dither = bits.astype(jnp.float32) * (1.0 / 65280.0) - 0.5
    return jnp.where(touched[:, None], updated + grid_step * dither, updated).astype(jnp.bfloat16)


def on_device(
    cold_table,
    cold_accum,
    dither_bits,
    hot_table,
    hot_accum,
    w_flat,
    w_inter,
    hidden_bias,
    w_out,
    targets,
    hot_ids,
    cold_slots,
    requests,
    counts,
):
    shards = lax.axis_size("shard")
    capacity = requests.shape[1]
    row_count = cold_table.shape[0]
    row_width = cold_table.shape[1]
    hot_count = hot_table.shape[0]
    cold_feats = cold_slots.shape[1]
    hot_grad = jnp.zeros((hot_count, row_width), jnp.float32)
    cold_grad = jnp.zeros((row_count, row_width), jnp.float32)
    touched = jnp.zeros((row_count,), jnp.float32)
    for micro_index in range(MB):
        asked_rows = requests[micro_index * shards : (micro_index + 1) * shards]
        requested = lax.all_to_all(asked_rows, "shard", split_axis=0, concat_axis=0, tiled=True)
        fetched_rows = lax.all_to_all(
            cold_table[requested], "shard", split_axis=0, concat_axis=0, tiled=True
        )
        first = micro_index * BATCH
        slot_part = cold_slots[first : first + BATCH]
        hot_part = hot_ids[first : first + BATCH]
        cold_vectors = fetched_rows.reshape(shards * capacity, row_width)[slot_part]
        stacked = jnp.concatenate([cold_vectors, hot_table[hot_part].astype(jnp.bfloat16)], axis=1)
        gradients = backprop(
            stacked, targets[first : first + BATCH], w_flat, w_inter, hidden_bias, w_out
        )
        slot_grad = jax.ops.segment_sum(
            gradients[:, :cold_feats].reshape(-1, row_width),
            slot_part.reshape(-1),
            num_segments=shards * capacity,
        )
        hot_term = jax.ops.segment_sum(
            gradients[:, cold_feats:].reshape(-1, row_width),
            hot_part.reshape(-1),
            num_segments=hot_count,
        )
        slot_grad, hot_term = (slot_grad.reshape(shards, capacity, row_width), hot_term)
        hot_grad = hot_grad + hot_term
        owner_grad, count_in = (
            lax.all_to_all(
                slot_grad.astype(jnp.bfloat16), "shard", split_axis=0, concat_axis=0, tiled=True
            ).astype(slot_grad.dtype),
            lax.all_to_all(counts[micro_index], "shard", split_axis=0, concat_axis=0, tiled=True),
        )
        cold_grad = cold_grad + jax.ops.segment_sum(
            owner_grad.reshape(-1, row_width), requested.reshape(-1), num_segments=row_count
        )
        live_mask = (jnp.arange(capacity, dtype=jnp.int32)[None, :] < count_in[:, None]).astype(
            jnp.float32
        )
        touched = touched + jax.ops.segment_sum(
            live_mask.reshape(-1), requested.reshape(-1), num_segments=row_count
        )
    summed_grad, summed_hits = (
        lax.psum(cold_grad.astype(jnp.bfloat16), "dp").astype(jnp.float32),
        lax.psum(touched.astype(jnp.bfloat16), "dp").astype(jnp.float32),
    )
    averaged = summed_grad / jnp.maximum(summed_hits, 1.0)[:, None]
    updated, cold_accum_out = adagrad_rows(cold_table.astype(jnp.float32), cold_accum, averaged)
    cold_out = requantize(updated, dither_bits, summed_hits > 0.5)
    total_hot = lax.psum(hot_grad, ("shard", "dp"))
    hot_out, hot_accum_out = adagrad_rows(hot_table, hot_accum, total_hot)
    return (cold_out, cold_accum_out, hot_out, hot_accum_out)


def solution(mesh):
    return jax.shard_map(
        on_device,
        mesh=mesh,
        in_specs=(
            P("shard", None),
            P("shard"),
            P("shard", None),
            P(),
            P(),
            P(),
            P(),
            P(),
            P(),
            P(("shard", "dp")),
            P(("shard", "dp"), None),
            P(("shard", "dp"), None),
            P(("shard", "dp"), None),
            P(("shard", "dp"), None),
        ),
        out_specs=(P("shard", None), P("shard"), P(), P()),
        check_vma=False,
    )
```

profile of v0, /device:TPU:8, one launch (start us, length us, event | category | flops | bytes accessed | tf_op | source)
XLA Modules:
  0.0 695.9 jit_solution(9611974366071185003)
XLA Ops:
  9.4 20.0 %all_to_all.62 = s32[32,1,64]{2,1,0:T(1,128)S(1)} all-to-all(s32[32,1,64]{2,1,0:T(1,128)S(1)} %bitcast.113), channel_id=1, replica_groups=mesh['shard'=32,'dp'=8] {'shard'}, dimensions={0} | all-to-all | bytes 16384 | tf_op jit(solution)/shard_map/all_to_all | solution.py:82
  29.4 4.9 all-to-all-start
  34.5 9.9 %gather_fusion.3 = bf16[2048,256]{1,0:T(8,128)(2,1)} fusion(bf16[2048,256]{1,0:T(8,128)(2,1)} %param.14, s32[2048]{0:T(1024)S(1)} %broadcast_clamp_fusion.3), kind=kCustom, calls=%fused_computation.3 | custom fusion | bytes 2105344 | tf_op jit(solution)/shard_map/gather | solution.py:84
  44.3 10.0 %all-to-all-start.6 = ((bf16[32,64,256]{2,1,0:T(8,128)(2,1)}), bf16[32,64,256]{2,1,0:T(8,128)(2,1)S(1)}, u32[]{:S(2)}, u32[]{:S(2)}) async-start(bf16[32,64,256]{2,1,0:T(8,128)(2,1)} %bitcast.16), calls=%async_computation.6 | async-start | bytes 2097152 | tf_op jit(solution)/shard_map/all_to_all | solution.py:83
  54.5 9.1 %gather_fusion = bf16[2048,256]{1,0:T(8,128)(2,1)} fusion(bf16[2048,256]{1,0:T(8,128)(2,1)S(1)} %copy-done.2, s32[2048]{0:T(1024)S(1)} %broadcast_clamp_fusion.5), kind=kCustom, calls=%fused_computation | custom fusion | bytes 2105344 | tf_op jit(solution)/shard_map/gather | solution.py:84
  63.5 17.2 %all-to-all-done.6 = bf16[32,64,256]{2,1,0:T(8,128)(2,1)S(1)} async-done(((bf16[32,64,256]{2,1,0:T(8,128)(2,1)}), bf16[32,64,256]{2,1,0:T(8,128)(2,1)S(1)}, u32[]{:S(2)}, u32[]{:S(2)}) %all-to-all-start.6) | async-done | bytes 1048608 | tf_op jit(solution)/shard_map/all_to_all | solution.py:83
  80.7 5.6 all-to-all-start.4
  98.1 8.4 %gather_fusion.5 = bf16[2048,256]{1,0:T(8,128)(2,1)} fusion(f32[1024,256]{1,0:T(8,128)S(1)} %copy-done.1, s32[2048]{0:T(1024)S(1)} %broadcast_clamp_fusion), kind=kCustom, calls=%fused_computation.5 | custom fusion | bytes 2105344 | tf_op jit(solution)/shard_map/gather | solution.py:90
  106.5 8.5 %gather_fusion.2 = bf16[2048,256]{1,0:T(8,128)(2,1)} fusion(f32[1024,256]{1,0:T(8,128)S(1)} %copy-done.1, s32[2048]{0:T(1024)S(1)} %broadcast_clamp_fusion.1), kind=kCustom, calls=%fused_computation.2 | custom fusion | bytes 2105344 | tf_op jit(solution)/shard_map/gather | solution.py:90
  115.0 9.0 %gather_fusion.4 = bf16[2048,256]{1,0:T(8,128)(2,1)} fusion(bf16[2048,256]{1,0:T(8,128)(2,1)S(1)} %bitcast.86, s32[2048]{0:T(1024)S(1)} %broadcast_clamp_fusion.2), kind=kCustom, calls=%fused_computation.4 | custom fusion | bytes 2105344 | tf_op jit(solution)/shard_map/gather | solution.py:89
  124.1 4.4 fusion.27
  129.9 10.5 %all-to-all-start.3 = ((s32[32,1,1]{2,1,0:T(1,128)}), s32[32,1,1]{2,1,0:T(1,128)}, u32[]{:S(2)}, u32[]{:S(2)}) async-start(s32[32,1,1]{2,1,0:T(1,128)} %copy.67), calls=%async_computation.3 | async-start | bytes 32768 | tf_op jit(solution)/shard_map/all_to_all | solution.py:110
  140.5 9.9 %gather_fusion.1 = bf16[2048,256]{1,0:T(8,128)(2,1)} fusion(bf16[2048,256]{1,0:T(8,128)(2,1)} %bitcast.6, s32[2048]{0:T(1024)S(1)} %broadcast_clamp_fusion.4), kind=kCustom, calls=%fused_computation.1 | custom fusion | bytes 2105344 | tf_op jit(solution)/shard_map/gather | solution.py:89
  150.3 4.3 fusion.28
  154.7 1.5 pad_maximum_fusion
  156.2 3.2 copy.77
  160.4 3.9 copy.84
  164.2 3.2 copy.71
  168.4 2.7 copy.82
  171.2 2.8 fusion.37
  177.6 3.2 fusion.35
  181.0 1.9 copy.73
  182.8 5.9 copy.83
  188.7 10.1 %all-to-all-start.1 = ((s32[32,1,1]{2,1,0:T(1,128)}), s32[32,1,1]{2,1,0:T(1,128)S(1)}, u32[]{:S(2)}, u32[]{:S(2)}) async-start(s32[32,1,1]{2,1,0:T(1,128)} %copy.66), calls=%async_computation.1 | async-start | bytes 32768 | tf_op jit(solution)/shard_map/all_to_all | solution.py:110
  198.8 5.8 bitcast_add_fusion.1
  204.6 13.5 %scatter_custom_fusion.2 = f32[2048,256]{1,0:T(8,128)} fusion(s32[2048]{0:T(1024)} %reshape.252, f32[256,16,256]{2,1,0:T(8,128)} %bitcast_add_fusion.1, f32[]{:T(128)} %constant.13.clone.1), kind=kCustom, calls=%fused_computation.25 | custom fusion | flops 524288 | bytes 4194816 | tf_op jit(solution)/shard_map/scatter-add | solution.py:94
  218.1 2.7 convert_element_type.84
  220.8 9.8 %all-to-all-start.5 = ((bf16[32,64,256]{2,1,0:T(8,128)(2,1)}), bf16[32,64,256]{2,1,0:T(8,128)(2,1)}, u32[]{:S(2)}, u32[]{:S(2)}) async-start(bf16[32,64,256]{2,1,0:T(8,128)(2,1)} %bitcast.104), calls=%async_computation.5 | async-start | bytes 2097152 | tf_op jit(solution)/shard_map/all_to_all | solution.py:107
  233.5 1.9 copy.79
  235.4 3.6 fusion.38
  239.0 1.8 copy.85
  240.8 2.9 bitcast_add_fusion
  243.7 13.6 %scatter_custom_fusion.4 = f32[2048,256]{1,0:T(8,128)} fusion(s32[2048]{0:T(1024)} %reshape.268, f32[256,16,256]{2,1,0:T(8,128)} %bitcast_add_fusion, f32[]{:T(128)} %constant.13.clone.1), kind=kCustom, calls=%fused_computation.23 | custom fusion | flops 524288 | bytes 4194816 | tf_op jit(solution)/shard_map/scatter-add | solution.py:94
  257.3 2.7 convert_element_type.90
  260.0 10.0 %all-to-all-start.7 = ((bf16[32,64,256]{2,1,0:T(8,128)(2,1)}), bf16[32,64,256]{2,1,0:T(8,128)(2,1)}, u32[]{:S(2)}, u32[]{:S(2)}) async-start(bf16[32,64,256]{2,1,0:T(8,128)(2,1)} %bitcast.24), calls=%async_computation.7 | async-start | bytes 2097152 | tf_op jit(solution)/shard_map/all_to_all | solution.py:107
  275.1 11.3 %scatter_custom_fusion.1 = f32[2048]{0:T(1024)S(1)} fusion(s32[2048]{0:T(1024)S(1)} %reshape.244, f32[2048]{0:T(1024)S(1)} %reshape.246, f32[]{:T(128)} %constant.13.clone.1), kind=kCustom, calls=%fused_computation.87 | custom fusion | flops 2048 | bytes 8196 | tf_op jit(solution)/shard_map/scatter-add | solution.py:118
  286.4 11.3 %scatter_custom_fusion = f32[2048]{0:T(1024)S(1)} fusion(s32[2048]{0:T(1024)S(1)} %reshape.236, f32[2048]{0:T(1024)S(1)} %reshape.238, f32[]{:T(128)} %constant.13.clone.1), kind=kCustom, calls=%fused_computation.89 | custom fusion | flops 2048 | bytes 8196 | tf_op jit(solution)/shard_map/scatter-add | solution.py:118
  297.7 12.4 %scatter_custom_fusion.6 = f32[1024,256]{1,0:T(8,128)S(1)} fusion(s32[2048]{0:T(1024)S(1)} %reshape.284, f32[256,16,256]{2,1,0:T(8,128)} %bitcast_add_fusion.1, f32[]{:T(128)} %constant.13.clone.1), kind=kCustom, calls=%fused_computation.21 | custom fusion | flops 524288 | bytes 3146240 | tf_op jit(solution)/shard_map/scatter-add | solution.py:99
  310.1 13.1 %scatter_custom_fusion.7 = f32[1024,256]{1,0:T(8,128)} fusion(s32[2048]{0:T(1024)S(1)} %reshape.292, f32[256,16,256]{2,1,0:T(8,128)} %bitcast_add_fusion, f32[]{:T(128)} %constant.13.clone.1), kind=kCustom, calls=%fused_computation.19 | custom fusion | flops 524288 | bytes 3146240 | tf_op jit(solution)/shard_map/scatter-add | solution.py:99
  323.2 2.3 add.148
  325.6 12.4 %psum.21 = bf16[2048]{0:T(1024)(128)(2,1)S(1)} all-reduce(bf16[2048]{0:T(1024)(128)(2,1)S(1)} %add_convert_fusion.1), channel_id=1, replica_groups=mesh['shard'=32,'dp'=8] {'dp'}, use_global_device_ids=true, to_apply=%region_2.0 | all-reduce | flops 2048 | bytes 8192 | tf_op jit(solution)/shard_map/psum | solution.py:123
  338.1 247.5 %all-reduce.5.cloned.1.call-done = f32[1024,256]{1,0:T(8,128)} async-done(((f32[1024,256]{1,0:T(8,128)}), f32[1024,256]{1,0:T(8,128)}) %all-reduce.5.cloned.1.call-update) | async-done | bytes 1048592 | tf_op jit(solution)/shard_map/psum | solution.py:128
  587.0 12.6 %scatter_custom_fusion.3 = f32[2048,256]{1,0:T(8,128)} fusion(s32[2048]{0:T(1024)S(1)} %reshape.236, bf16[2048,256]{1,0:T(8,128)(2,1)} %bitcast.28, f32[]{:T(128)} %constant.13.clone.1), kind=kCustom, calls=%fused_computation.30 | custom fusion | flops 1048576 | bytes 3145732 | tf_op jit(solution)/shard_map/scatter-add | solution.py:112
  599.6 12.3 %scatter_custom_fusion.5 = f32[2048,256]{1,0:T(8,128)} fusion(s32[2048]{0:T(1024)S(1)} %reshape.244, bf16[2048,256]{1,0:T(8,128)(2,1)} %bitcast.29, f32[]{:T(128)} %constant.13.clone.1), kind=kCustom, calls=%fused_computation.28 | custom fusion | flops 1048576 | bytes 3145732 | tf_op jit(solution)/shard_map/scatter-add | solution.py:112
  611.9 3.5 add_convert_fusion
  617.3 64.7 %all-reduce.3.cloned.1.call-done = bf16[2048,256]{1,0:T(8,128)(2,1)} async-done(((bf16[2048,256]{1,0:T(8,128)(2,1)}), bf16[2048,256]{1,0:T(8,128)(2,1)}) %all-reduce.3.cloned.1.call-update) | async-done | bytes 1048592 | tf_op jit(solution)/shard_map/psum | solution.py:122
  681.9 1.9 multiply_reduce_fusion
  684.5 2.2 abs_reduce_fusion
  (130 shorter events, 33.9 us)
Async XLA Ops:
  8.0 167.3 %copy-start = (bf16[256,512]{1,0:T(8,128)(2,1)S(1)}, bf16[256,512]{1,0:T(8,128)(2,1)}, u32[]{:S(2)}) copy-start(bf16[256,512]{1,0:T(8,128)(2,1)} %param.20) | copy-start | bytes 786436
  29.4 14.9 %copy-start.12 = (s32[32,1,64]{2,1,0:T(1,128)}, s32[32,1,64]{2,1,0:T(1,128)S(1)}, u32[]{:S(2)}) copy-start(s32[32,1,64]{2,1,0:T(1,128)S(1)} %all_to_all.62) | copy-start | bytes 24580
  29.4 14.9 %all-to-all-start = ((s32[32,1,64]{2,1,0:T(1,128)}), s32[32,1,64]{2,1,0:T(1,128)S(1)}, u32[]{:S(2)}, u32[]{:S(2)}) async-start(s32[32,1,64]{2,1,0:T(1,128)} %bitcast), calls=%async_computation | async-start | bytes 32768 | tf_op jit(solution)/shard_map/all_to_all | solution.py:82
  44.3 10.1 %copy-start.2 = (bf16[2048,256]{1,0:T(8,128)(2,1)S(1)}, bf16[2048,256]{1,0:T(8,128)(2,1)}, u32[]{:S(2)}) copy-start(bf16[2048,256]{1,0:T(8,128)(2,1)} %param.14) | copy-start | bytes 3145732
  44.3 36.4 %all-to-all-start.6 = ((bf16[32,64,256]{2,1,0:T(8,128)(2,1)}), bf16[32,64,256]{2,1,0:T(8,128)(2,1)S(1)}, u32[]{:S(2)}, u32[]{:S(2)}) async-start(bf16[32,64,256]{2,1,0:T(8,128)(2,1)} %bitcast.16), calls=%async_computation.6 | async-start | bytes 2097152 | tf_op jit(solution)/shard_map/all_to_all | solution.py:83
  63.5 22.8 %copy-start.27 = (s32[2,32]{1,0:T(2,128)S(1)}, s32[2,32]{1,0:T(2,128)}, u32[]{:S(2)}) copy-start(s32[2,32]{1,0:T(2,128)} %param.27) | copy-start | bytes 772
  63.5 24.2 %copy-start.21 = (s32[512,8]{0,1:T(8,128)S(1)}, s32[512,8]{0,1:T(8,128)}, u32[]{:S(2)}) copy-start(s32[512,8]{0,1:T(8,128)} %param.25) | copy-start | bytes 49156
  63.5 34.5 %copy-start.1 = (f32[1024,256]{1,0:T(8,128)S(1)}, f32[1024,256]{1,0:T(8,128)}, u32[]{:S(2)}) copy-start(f32[1024,256]{1,0:T(8,128)} %param.17) | copy-start | bytes 3145732
  80.7 49.2 %all-to-all-start.4 = ((bf16[32,64,256]{2,1,0:T(8,128)(2,1)}), bf16[32,64,256]{2,1,0:T(8,128)(2,1)}, u32[]{:S(2)}, u32[]{:S(2)}) async-start(bf16[32,64,256]{2,1,0:T(8,128)(2,1)} %bitcast.103), calls=%async_computation.4 | async-start | bytes 2097152 | tf_op jit(solution)/shard_map/all_to_all | solution.py:83
  98.1 8.4 %copy-start.18 = (s32[2048]{0:T(1024)S(1)}, s32[2048]{0:T(1024)}, u32[]{:S(2)}) copy-start(s32[2048]{0:T(1024)} %reshape.204) | copy-start | bytes 24580
  106.5 8.5 %copy-start.16 = (s32[2048]{0:T(1024)S(1)}, s32[2048]{0:T(1024)}, u32[]{:S(2)}) copy-start(s32[2048]{0:T(1024)} %reshape.196) | copy-start | bytes 24580
  106.5 8.5 %copy-start.17 = (s32[2048]{0:T(1024)S(1)}, s32[2048]{0:T(1024)}, u32[]{:S(2)}) copy-start(s32[2048]{0:T(1024)} %reshape.220) | copy-start | bytes 24580
  124.0 4.4 copy-start.4
  124.0 4.4 copy-start.5
  129.9 58.8 %all-to-all-start.3 = ((s32[32,1,1]{2,1,0:T(1,128)}), s32[32,1,1]{2,1,0:T(1,128)}, u32[]{:S(2)}, u32[]{:S(2)}) async-start(s32[32,1,1]{2,1,0:T(1,128)} %copy.67), calls=%async_computation.3 | async-start | bytes 32768 | tf_op jit(solution)/shard_map/all_to_all | solution.py:110
  150.3 4.3 copy-start.7
  150.3 4.3 copy-start.8
  168.4 2.8 copy-start.3
  174.1 1.3 copy-start.24
  174.1 1.5 copy-start.25
  175.6 0.7 copy-start.26
  188.7 32.0 %all-to-all-start.1 = ((s32[32,1,1]{2,1,0:T(1,128)}), s32[32,1,1]{2,1,0:T(1,128)S(1)}, u32[]{:S(2)}, u32[]{:S(2)}) async-start(s32[32,1,1]{2,1,0:T(1,128)} %copy.66), calls=%async_computation.1 | async-start | bytes 32768 | tf_op jit(solution)/shard_map/all_to_all | solution.py:110
  220.8 9.8 %copy-start.14 = (s32[32,1,1]{2,1,0:T(1,128)}, s32[32,1,1]{2,1,0:T(1,128)S(1)}, u32[]{:S(2)}) copy-start(s32[32,1,1]{2,1,0:T(1,128)S(1)} %all-to-all-done.1) | copy-start | bytes 388
  220.8 39.2 %all-to-all-start.5 = ((bf16[32,64,256]{2,1,0:T(8,128)(2,1)}), bf16[32,64,256]{2,1,0:T(8,128)(2,1)}, u32[]{:S(2)}, u32[]{:S(2)}) async-start(bf16[32,64,256]{2,1,0:T(8,128)(2,1)} %bitcast.104), calls=%async_computation.5 | async-start | bytes 2097152 | tf_op jit(solution)/shard_map/all_to_all | solution.py:107
  239.0 1.8 copy-start.6
  239.0 1.8 copy-start.10
  257.3 12.9 %copy-start.20 = (s32[256,8]{0,1:T(8,128)S(1)}, s32[256,8]{0,1:T(8,128)}, u32[]{:S(2)}) copy-start(s32[256,8]{0,1:T(8,128)} %get-tuple-element.14) | copy-start | bytes 24580
  257.3 13.2 %copy-start.19 = (s32[256,8]{0,1:T(8,128)S(1)}, s32[256,8]{0,1:T(8,128)}, u32[]{:S(2)}) copy-start(s32[256,8]{0,1:T(8,128)} %get-tuple-element.17) | copy-start | bytes 24580
  260.0 12.3 %copy-start.15 = (s32[32,1,1]{2,1,0:T(1,128)S(1)}, s32[32,1,1]{2,1,0:T(1,128)}, u32[]{:S(2)}) copy-start(s32[32,1,1]{2,1,0:T(1,128)} %copy-done.14) | copy-start | bytes 388
  260.0 13.6 %copy-start.13 = (s32[32,1,64]{2,1,0:T(1,128)S(1)}, s32[32,1,64]{2,1,0:T(1,128)}, u32[]{:S(2)}) copy-start(s32[32,1,64]{2,1,0:T(1,128)} %copy-done.12) | copy-start | bytes 24580
  260.0 339.7 %all-to-all-start.7 = ((bf16[32,64,256]{2,1,0:T(8,128)(2,1)}), bf16[32,64,256]{2,1,0:T(8,128)(2,1)}, u32[]{:S(2)}, u32[]{:S(2)}) async-start(bf16[32,64,256]{2,1,0:T(8,128)(2,1)} %bitcast.24), calls=%async_computation.7 | async-start | bytes 2097152 | tf_op jit(solution)/shard_map/all_to_all | solution.py:107
  269.9 315.6 %all-reduce.5.cloned.1.call-start = ((), (), s32[]{:S(2)}) async-start(), calls=%async_computation.9 | async-start | bytes 2097152 | tf_op jit(solution)/shard_map/psum | solution.py:128
  325.5 356.4 %all-reduce.3.cloned.1.call-start = ((), (), s32[]{:S(2)}) async-start(), calls=%async_computation.8 | async-start | bytes 2097152 | tf_op jit(solution)/shard_map/psum | solution.py:122
  611.9 3.5 copy-start.23
  611.9 4.1 copy-start.9
  616.1 67.8 %copy-start.22 = (f32[2048]{0:T(1024)S(1)}, f32[2048]{0:T(1024)}, u32[]{:S(2)}) copy-start(f32[2048]{0:T(1024)} %param.15) | copy-start | bytes 24580
  684.5 2.2 copy-start.11
Sparse Core Ops, SparseCore 0:
  325.6 259.8 all-reduce.4
Sparse Core Ops, SparseCore 1:
  615.5 66.3 all-reduce.2
where the time goes:
time: 702 us; the launch traced here: 696 us
  waiting for transfers between devices  329 us (47%)
  other arithmetic  133 us (19%)
  local copies, waits for them, and re-layouts  92.7 us (13%)
  starting transfers between devices  61.3 us (9%)
  blocking collectives  32.5 us (5%)
  matrix products  30.5 us (4%)
  between operations  16.3 us (2%)
    psum x1, waiting for transfers between devices, on_device(): total_hot = lax.psum(hot_grad, ('shard', 'dp'))  248 us
    psum x1, waiting for transfers between devices, on_device(): lax.psum(cold_grad.astype(jnp.bfloat16), 'dp').astype(jnp.float32)  64.7 us
    scatter-add x2, other arithmetic, on_device(): jax.ops.segment_sum(gradients[:, :cold_feats].reshape(-1, row_width), slo...  27.1 us
    scatter-add x2, other arithmetic, on_device(): jax.ops.segment_sum(gradients[:, cold_feats:].reshape(-1, row_width), hot...  25.5 us
    scatter-add x2, other arithmetic, on_device(): jax.ops.segment_sum(owner_grad.reshape(-1, row_width), requested.reshape(...  24.9 us
    scatter-add x2, other arithmetic, on_device(): jax.ops.segment_sum(live_mask.reshape(-1), requested.reshape(-1), num_seg...  22.6 us
    all_to_all x2, starting transfers between devices, on_device(): lax.all_to_all(counts[micro_index], 'shard', split_axis=0, concat_axis=0,...  20.6 us
    all_to_all x1, blocking collectives, on_device(): lax.all_to_all(asked_rows, 'shard', split_axis=0, concat_axis=0, tiled=True)  20 us
  transfers between devices with their start and end apart: 9, of which 3 were waited for; matrix products, arithmetic and copies ran while one was open for 33% of the time, Pallas kernels for 0%

commit v1 on v0

--- a/solution.py
+++ b/solution.py
@@ -125,7 +125,9 @@
     averaged = summed_grad / jnp.maximum(summed_hits, 1.0)[:, None]
     updated, cold_accum_out = adagrad_rows(cold_table.astype(jnp.float32), cold_accum, averaged)
     cold_out = requantize(updated, dither_bits, summed_hits > 0.5)
-    total_hot = lax.psum(hot_grad, ("shard", "dp"))
+    total_hot = hot_grad
+    for over in ("shard", "dp"):
+        total_hot = lax.psum(total_hot, over)
     hot_out, hot_accum_out = adagrad_rows(hot_table, hot_accum, total_hot)
     return (cold_out, cold_accum_out, hot_out, hot_accum_out)
 

time: 702 us -> 633 us (0.902)
  waiting for transfers between devices: 329 us -> 262 us
    psum x1 -> x2, waiting for transfers between devices: 248 us -> 179 us  [on_device(): total_hot = lax.psum(total_hot, over)]
  transfers between devices with their start and end apart: 9 -> 10, of which waited for: 3 -> 4; matrix products, arithmetic and copies ran while one was open for 33% -> 37% of each run, Pallas kernels for 0% -> 0%
where the time goes in v1:
time: 633 us; the launch traced here: 627 us
  waiting for transfers between devices  262 us (41%)
  other arithmetic  133 us (21%)
  local copies, waits for them, and re-layouts  92.7 us (15%)
  starting transfers between devices  61.2 us (10%)
  blocking collectives  32.5 us (5%)
  matrix products  30.5 us (5%)
  between operations  14.6 us (2%)
    psum x2, waiting for transfers between devices, on_device(): total_hot = lax.psum(total_hot, over)  179 us
    psum x1, waiting for transfers between devices, on_device(): lax.psum(cold_grad.astype(jnp.bfloat16), 'dp').astype(jnp.float32)  65.4 us
    scatter-add x2, other arithmetic, on_device(): jax.ops.segment_sum(gradients[:, :cold_feats].reshape(-1, row_width), slo...  27.1 us
    scatter-add x2, other arithmetic, on_device(): jax.ops.segment_sum(gradients[:, cold_feats:].reshape(-1, row_width), hot...  25.5 us
    scatter-add x2, other arithmetic, on_device(): jax.ops.segment_sum(owner_grad.reshape(-1, row_width), requested.reshape(...  24.9 us
    scatter-add x2, other arithmetic, on_device(): jax.ops.segment_sum(live_mask.reshape(-1), requested.reshape(-1), num_seg...  22.6 us
    all_to_all x2, starting transfers between devices, on_device(): lax.all_to_all(counts[micro_index], 'shard', split_axis=0, concat_axis=0,...  20.6 us
    all_to_all x1, blocking collectives, on_device(): lax.all_to_all(asked_rows, 'shard', split_axis=0, concat_axis=0, tiled=True)  20 us
  transfers between devices with their start and end apart: 10, of which 4 were waited for; matrix products, arithmetic and copies ran while one was open for 37% of the time, Pallas kernels for 0%

profile of v1, /device:TPU:8, one launch (start us, length us, event | category | flops | bytes accessed | tf_op | source)
XLA Modules:
  0.0 626.7 jit_solution(16338508620922170230)
XLA Ops:
  8.6 20.0 %all_to_all.62 = s32[32,1,64]{2,1,0:T(1,128)S(1)} all-to-all(s32[32,1,64]{2,1,0:T(1,128)S(1)} %bitcast.113), channel_id=1, replica_groups=mesh['shard'=32,'dp'=8] {'shard'}, dimensions={0} | all-to-all | bytes 16384 | tf_op jit(solution)/shard_map/all_to_all | solution.py:82
  28.6 4.9 all-to-all-start
  33.6 9.9 %gather_fusion.3 = bf16[2048,256]{1,0:T(8,128)(2,1)} fusion(bf16[2048,256]{1,0:T(8,128)(2,1)} %param.14, s32[2048]{0:T(1024)S(1)} %broadcast_clamp_fusion.3), kind=kCustom, calls=%fused_computation.3 | custom fusion | bytes 2105344 | tf_op jit(solution)/shard_map/gather | solution.py:84
  43.5 10.0 %all-to-all-start.6 = ((bf16[32,64,256]{2,1,0:T(8,128)(2,1)}), bf16[32,64,256]{2,1,0:T(8,128)(2,1)S(1)}, u32[]{:S(2)}, u32[]{:S(2)}) async-start(bf16[32,64,256]{2,1,0:T(8,128)(2,1)} %bitcast.16), calls=%async_computation.6 | async-start | bytes 2097152 | tf_op jit(solution)/shard_map/all_to_all | solution.py:83
  53.6 9.1 %gather_fusion = bf16[2048,256]{1,0:T(8,128)(2,1)} fusion(bf16[2048,256]{1,0:T(8,128)(2,1)S(1)} %copy-done.2, s32[2048]{0:T(1024)S(1)} %broadcast_clamp_fusion.5), kind=kCustom, calls=%fused_computation | custom fusion | bytes 2105344 | tf_op jit(solution)/shard_map/gather | solution.py:84
  62.7 17.2 %all-to-all-done.6 = bf16[32,64,256]{2,1,0:T(8,128)(2,1)S(1)} async-done(((bf16[32,64,256]{2,1,0:T(8,128)(2,1)}), bf16[32,64,256]{2,1,0:T(8,128)(2,1)S(1)}, u32[]{:S(2)}, u32[]{:S(2)}) %all-to-all-start.6) | async-done | bytes 1048608 | tf_op jit(solution)/shard_map/all_to_all | solution.py:83
  79.9 5.6 all-to-all-start.4
  97.2 8.4 %gather_fusion.5 = bf16[2048,256]{1,0:T(8,128)(2,1)} fusion(f32[1024,256]{1,0:T(8,128)S(1)} %copy-done.1, s32[2048]{0:T(1024)S(1)} %broadcast_clamp_fusion), kind=kCustom, calls=%fused_computation.5 | custom fusion | bytes 2105344 | tf_op jit(solution)/shard_map/gather | solution.py:90
  105.7 8.5 %gather_fusion.2 = bf16[2048,256]{1,0:T(8,128)(2,1)} fusion(f32[1024,256]{1,0:T(8,128)S(1)} %copy-done.1, s32[2048]{0:T(1024)S(1)} %broadcast_clamp_fusion.1), kind=kCustom, calls=%fused_computation.2 | custom fusion | bytes 2105344 | tf_op jit(solution)/shard_map/gather | solution.py:90
  114.2 9.0 %gather_fusion.4 = bf16[2048,256]{1,0:T(8,128)(2,1)} fusion(bf16[2048,256]{1,0:T(8,128)(2,1)S(1)} %bitcast.86, s32[2048]{0:T(1024)S(1)} %broadcast_clamp_fusion.2), kind=kCustom, calls=%fused_computation.4 | custom fusion | bytes 2105344 | tf_op jit(solution)/shard_map/gather | solution.py:89
  123.2 4.4 fusion.27
  129.1 10.5 %all-to-all-start.3 = ((s32[32,1,1]{2,1,0:T(1,128)}), s32[32,1,1]{2,1,0:T(1,128)}, u32[]{:S(2)}, u32[]{:S(2)}) async-start(s32[32,1,1]{2,1,0:T(1,128)} %copy.67), calls=%async_computation.3 | async-start | bytes 32768 | tf_op jit(solution)/shard_map/all_to_all | solution.py:110
  139.6 9.9 %gather_fusion.1 = bf16[2048,256]{1,0:T(8,128)(2,1)} fusion(bf16[2048,256]{1,0:T(8,128)(2,1)} %bitcast.6, s32[2048]{0:T(1024)S(1)} %broadcast_clamp_fusion.4), kind=kCustom, calls=%fused_computation.1 | custom fusion | bytes 2105344 | tf_op jit(solution)/shard_map/gather | solution.py:89
  149.5 4.3 fusion.28
  155.4 3.2 copy.77
  159.5 3.9 copy.84
  163.4 3.2 copy.71
  167.6 2.7 copy.82
  170.4 2.8 fusion.37
  176.8 3.2 fusion.35
  180.1 1.9 copy.73
  182.0 5.9 copy.83
  187.9 10.1 %all-to-all-start.1 = ((s32[32,1,1]{2,1,0:T(1,128)}), s32[32,1,1]{2,1,0:T(1,128)S(1)}, u32[]{:S(2)}, u32[]{:S(2)}) async-start(s32[32,1,1]{2,1,0:T(1,128)} %copy.66), calls=%async_computation.1 | async-start | bytes 32768 | tf_op jit(solution)/shard_map/all_to_all | solution.py:110
  198.0 5.8 bitcast_add_fusion.1
  203.7 13.5 %scatter_custom_fusion.2 = f32[2048,256]{1,0:T(8,128)} fusion(s32[2048]{0:T(1024)} %reshape.252, f32[256,16,256]{2,1,0:T(8,128)} %bitcast_add_fusion.1, f32[]{:T(128)} %constant.13.clone.1), kind=kCustom, calls=%fused_computation.25 | custom fusion | flops 524288 | bytes 4194816 | tf_op jit(solution)/shard_map/scatter-add | solution.py:94
  217.2 2.7 convert_element_type.84
  219.9 9.8 %all-to-all-start.5 = ((bf16[32,64,256]{2,1,0:T(8,128)(2,1)}), bf16[32,64,256]{2,1,0:T(8,128)(2,1)}, u32[]{:S(2)}, u32[]{:S(2)}) async-start(bf16[32,64,256]{2,1,0:T(8,128)(2,1)} %bitcast.104), calls=%async_computation.5 | async-start | bytes 2097152 | tf_op jit(solution)/shard_map/all_to_all | solution.py:107
  232.7 1.9 copy.79
  234.5 3.6 fusion.38
  238.1 1.8 copy.85
  239.9 2.9 bitcast_add_fusion
  242.8 13.6 %scatter_custom_fusion.4 = f32[2048,256]{1,0:T(8,128)} fusion(s32[2048]{0:T(1024)} %reshape.268, f32[256,16,256]{2,1,0:T(8,128)} %bitcast_add_fusion, f32[]{:T(128)} %constant.13.clone.1), kind=kCustom, calls=%fused_computation.23 | custom fusion | flops 524288 | bytes 4194816 | tf_op jit(solution)/shard_map/scatter-add | solution.py:94
  256.4 2.7 convert_element_type.90
  259.1 9.8 %all-to-all-start.7 = ((bf16[32,64,256]{2,1,0:T(8,128)(2,1)}), bf16[32,64,256]{2,1,0:T(8,128)(2,1)}, u32[]{:S(2)}, u32[]{:S(2)}) async-start(bf16[32,64,256]{2,1,0:T(8,128)(2,1)} %bitcast.24), calls=%async_computation.7 | async-start | bytes 2097152 | tf_op jit(solution)/shard_map/all_to_all | solution.py:107
  269.7 12.4 %scatter_custom_fusion.6 = f32[1024,256]{1,0:T(8,128)S(1)} fusion(s32[2048]{0:T(1024)S(1)} %reshape.284, f32[256,16,256]{2,1,0:T(8,128)} %bitcast_add_fusion.1, f32[]{:T(128)} %constant.13.clone.1), kind=kCustom, calls=%fused_computation.21 | custom fusion | flops 524288 | bytes 3146240 | tf_op jit(solution)/shard_map/scatter-add | solution.py:99
  282.1 13.1 %scatter_custom_fusion.7 = f32[1024,256]{1,0:T(8,128)} fusion(s32[2048]{0:T(1024)S(1)} %reshape.292, f32[256,16,256]{2,1,0:T(8,128)} %bitcast_add_fusion, f32[]{:T(128)} %constant.13.clone.1), kind=kCustom, calls=%fused_computation.19 | custom fusion | flops 524288 | bytes 3146240 | tf_op jit(solution)/shard_map/scatter-add | solution.py:99
  295.2 2.3 add.150
  302.0 11.3 %scatter_custom_fusion.1 = f32[2048]{0:T(1024)S(1)} fusion(s32[2048]{0:T(1024)S(1)} %reshape.244, f32[2048]{0:T(1024)S(1)} %reshape.246, f32[]{:T(128)} %constant.13.clone.1), kind=kCustom, calls=%fused_computation.87 | custom fusion | flops 2048 | bytes 8196 | tf_op jit(solution)/shard_map/scatter-add | solution.py:118
  313.3 11.3 %scatter_custom_fusion = f32[2048]{0:T(1024)S(1)} fusion(s32[2048]{0:T(1024)S(1)} %reshape.236, f32[2048]{0:T(1024)S(1)} %reshape.238, f32[]{:T(128)} %constant.13.clone.1), kind=kCustom, calls=%fused_computation.89 | custom fusion | flops 2048 | bytes 8196 | tf_op jit(solution)/shard_map/scatter-add | solution.py:118
  324.6 123.2 %all-reduce.6.cloned.1.call-done = f32[1024,256]{1,0:T(8,128)} async-done(((f32[1024,256]{1,0:T(8,128)}), f32[1024,256]{1,0:T(8,128)}) %all-reduce.6.cloned.1.call-update) | async-done | bytes 1048592 | tf_op jit(solution)/shard_map/psum | solution.py:130
  447.9 12.4 %psum.28 = bf16[2048]{0:T(1024)(128)(2,1)S(1)} all-reduce(bf16[2048]{0:T(1024)(128)(2,1)S(1)} %add_convert_fusion.1), channel_id=1, replica_groups=mesh['shard'=32,'dp'=8] {'dp'}, use_global_device_ids=true, to_apply=%region_2.0 | all-reduce | flops 2048 | bytes 8192 | tf_op jit(solution)/shard_map/psum | solution.py:123
  460.4 56.2 %all-reduce.8.cloned.1.call-done = f32[1024,256]{1,0:T(8,128)} async-done(((f32[1024,256]{1,0:T(8,128)}), f32[1024,256]{1,0:T(8,128)}) %all-reduce.8.cloned.1.call-update) | async-done | bytes 1048592 | tf_op jit(solution)/shard_map/psum | solution.py:130
  518.0 12.6 %scatter_custom_fusion.3 = f32[2048,256]{1,0:T(8,128)} fusion(s32[2048]{0:T(1024)S(1)} %reshape.236, bf16[2048,256]{1,0:T(8,128)(2,1)} %bitcast.28, f32[]{:T(128)} %constant.13.clone.1), kind=kCustom, calls=%fused_computation.30 | custom fusion | flops 1048576 | bytes 3145732 | tf_op jit(solution)/shard_map/scatter-add | solution.py:112
  530.6 12.3 %scatter_custom_fusion.5 = f32[2048,256]{1,0:T(8,128)} fusion(s32[2048]{0:T(1024)S(1)} %reshape.244, bf16[2048,256]{1,0:T(8,128)(2,1)} %bitcast.29, f32[]{:T(128)} %constant.13.clone.1), kind=kCustom, calls=%fused_computation.28 | custom fusion | flops 1048576 | bytes 3145732 | tf_op jit(solution)/shard_map/scatter-add | solution.py:112
  542.9 3.5 add_convert_fusion
  548.2 65.4 %all-reduce.4.cloned.1.call-done = bf16[2048,256]{1,0:T(8,128)(2,1)} async-done(((bf16[2048,256]{1,0:T(8,128)(2,1)}), bf16[2048,256]{1,0:T(8,128)(2,1)}) %all-reduce.4.cloned.1.call-update) | async-done | bytes 1048592 | tf_op jit(solution)/shard_map/psum | solution.py:122
  613.7 1.9 multiply_reduce_fusion
  616.2 2.2 abs_reduce_fusion
  (133 shorter events, 35.5 us)
Async XLA Ops:
  7.2 167.3 %copy-start = (bf16[256,512]{1,0:T(8,128)(2,1)S(1)}, bf16[256,512]{1,0:T(8,128)(2,1)}, u32[]{:S(2)}) copy-start(bf16[256,512]{1,0:T(8,128)(2,1)} %param.20) | copy-start | bytes 786436
  28.6 14.9 %copy-start.12 = (s32[32,1,64]{2,1,0:T(1,128)}, s32[32,1,64]{2,1,0:T(1,128)S(1)}, u32[]{:S(2)}) copy-start(s32[32,1,64]{2,1,0:T(1,128)S(1)} %all_to_all.62) | copy-start | bytes 24580
  28.6 14.9 %all-to-all-start = ((s32[32,1,64]{2,1,0:T(1,128)}), s32[32,1,64]{2,1,0:T(1,128)S(1)}, u32[]{:S(2)}, u32[]{:S(2)}) async-start(s32[32,1,64]{2,1,0:T(1,128)} %bitcast), calls=%async_computation | async-start | bytes 32768 | tf_op jit(solution)/shard_map/all_to_all | solution.py:82
  43.5 10.1 %copy-start.2 = (bf16[2048,256]{1,0:T(8,128)(2,1)S(1)}, bf16[2048,256]{1,0:T(8,128)(2,1)}, u32[]{:S(2)}) copy-start(bf16[2048,256]{1,0:T(8,128)(2,1)} %param.14) | copy-start | bytes 3145732
  43.5 36.4 %all-to-all-start.6 = ((bf16[32,64,256]{2,1,0:T(8,128)(2,1)}), bf16[32,64,256]{2,1,0:T(8,128)(2,1)S(1)}, u32[]{:S(2)}, u32[]{:S(2)}) async-start(bf16[32,64,256]{2,1,0:T(8,128)(2,1)} %bitcast.16), calls=%async_computation.6 | async-start | bytes 2097152 | tf_op jit(solution)/shard_map/all_to_all | solution.py:83
  62.7 22.8 %copy-start.27 = (s32[2,32]{1,0:T(2,128)S(1)}, s32[2,32]{1,0:T(2,128)}, u32[]{:S(2)}) copy-start(s32[2,32]{1,0:T(2,128)} %param.27) | copy-start | bytes 772
  62.7 24.2 %copy-start.21 = (s32[512,8]{0,1:T(8,128)S(1)}, s32[512,8]{0,1:T(8,128)}, u32[]{:S(2)}) copy-start(s32[512,8]{0,1:T(8,128)} %param.25) | copy-start | bytes 49156
  62.7 34.5 %copy-start.1 = (f32[1024,256]{1,0:T(8,128)S(1)}, f32[1024,256]{1,0:T(8,128)}, u32[]{:S(2)}) copy-start(f32[1024,256]{1,0:T(8,128)} %param.17) | copy-start | bytes 3145732
  79.9 49.2 %all-to-all-start.4 = ((bf16[32,64,256]{2,1,0:T(8,128)(2,1)}), bf16[32,64,256]{2,1,0:T(8,128)(2,1)}, u32[]{:S(2)}, u32[]{:S(2)}) async-start(bf16[32,64,256]{2,1,0:T(8,128)(2,1)} %bitcast.103), calls=%async_computation.4 | async-start | bytes 2097152 | tf_op jit(solution)/shard_map/all_to_all | solution.py:83
  97.2 8.4 %copy-start.18 = (s32[2048]{0:T(1024)S(1)}, s32[2048]{0:T(1024)}, u32[]{:S(2)}) copy-start(s32[2048]{0:T(1024)} %reshape.204) | copy-start | bytes 24580
  105.7 8.5 %copy-start.16 = (s32[2048]{0:T(1024)S(1)}, s32[2048]{0:T(1024)}, u32[]{:S(2)}) copy-start(s32[2048]{0:T(1024)} %reshape.196) | copy-start | bytes 24580
  105.7 8.5 %copy-start.17 = (s32[2048]{0:T(1024)S(1)}, s32[2048]{0:T(1024)}, u32[]{:S(2)}) copy-start(s32[2048]{0:T(1024)} %reshape.220) | copy-start | bytes 24580
  123.2 4.4 copy-start.4
  123.2 4.4 copy-start.5
  129.1 58.8 %all-to-all-start.3 = ((s32[32,1,1]{2,1,0:T(1,128)}), s32[32,1,1]{2,1,0:T(1,128)}, u32[]{:S(2)}, u32[]{:S(2)}) async-start(s32[32,1,1]{2,1,0:T(1,128)} %copy.67), calls=%async_computation.3 | async-start | bytes 32768 | tf_op jit(solution)/shard_map/all_to_all | solution.py:110
  149.5 4.3 copy-start.7
  149.5 4.3 copy-start.8
  167.6 2.8 copy-start.3
  173.2 1.3 copy-start.24
  173.2 1.5 copy-start.25
  174.8 0.7 copy-start.26
  187.9 32.0 %all-to-all-start.1 = ((s32[32,1,1]{2,1,0:T(1,128)}), s32[32,1,1]{2,1,0:T(1,128)S(1)}, u32[]{:S(2)}, u32[]{:S(2)}) async-start(s32[32,1,1]{2,1,0:T(1,128)} %copy.66), calls=%async_computation.1 | async-start | bytes 32768 | tf_op jit(solution)/shard_map/all_to_all | solution.py:110
  219.9 9.8 %copy-start.14 = (s32[32,1,1]{2,1,0:T(1,128)}, s32[32,1,1]{2,1,0:T(1,128)S(1)}, u32[]{:S(2)}) copy-start(s32[32,1,1]{2,1,0:T(1,128)S(1)} %all-to-all-done.1) | copy-start | bytes 388
  219.9 39.2 %all-to-all-start.5 = ((bf16[32,64,256]{2,1,0:T(8,128)(2,1)}), bf16[32,64,256]{2,1,0:T(8,128)(2,1)}, u32[]{:S(2)}, u32[]{:S(2)}) async-start(bf16[32,64,256]{2,1,0:T(8,128)(2,1)} %bitcast.104), calls=%async_computation.5 | async-start | bytes 2097152 | tf_op jit(solution)/shard_map/all_to_all | solution.py:107
  238.1 1.8 copy-start.6
  238.1 1.8 copy-start.10
  256.4 12.8 %copy-start.20 = (s32[256,8]{0,1:T(8,128)S(1)}, s32[256,8]{0,1:T(8,128)}, u32[]{:S(2)}) copy-start(s32[256,8]{0,1:T(8,128)} %get-tuple-element.14) | copy-start | bytes 24580
  256.4 13.1 %copy-start.19 = (s32[256,8]{0,1:T(8,128)S(1)}, s32[256,8]{0,1:T(8,128)}, u32[]{:S(2)}) copy-start(s32[256,8]{0,1:T(8,128)} %get-tuple-element.17) | copy-start | bytes 24580
  259.1 271.5 %all-to-all-start.7 = ((bf16[32,64,256]{2,1,0:T(8,128)(2,1)}), bf16[32,64,256]{2,1,0:T(8,128)(2,1)}, u32[]{:S(2)}, u32[]{:S(2)}) async-start(bf16[32,64,256]{2,1,0:T(8,128)(2,1)} %bitcast.24), calls=%async_computation.7 | async-start | bytes 2097152 | tf_op jit(solution)/shard_map/all_to_all | solution.py:107
  269.0 178.9 %all-reduce.6.cloned.1.call-start = ((), (), s32[]{:S(2)}) async-start(), calls=%async_computation.9 | async-start | bytes 2097152 | tf_op jit(solution)/shard_map/psum | solution.py:130
  295.2 4.0 copy-start.15
  295.2 5.3 copy-start.13
  297.6 218.9 %all-reduce.8.cloned.1.call-start = ((), (), s32[]{:S(2)}) async-start(), calls=%async_computation.10 | async-start | bytes 2097152 | tf_op jit(solution)/shard_map/psum | solution.py:130
  447.8 165.8 %all-reduce.4.cloned.1.call-start = ((), (), s32[]{:S(2)}) async-start(), calls=%async_computation.8 | async-start | bytes 2097152 | tf_op jit(solution)/shard_map/psum | solution.py:122
  542.9 3.5 copy-start.23
  542.9 4.1 copy-start.9
  547.0 68.5 %copy-start.22 = (f32[2048]{0:T(1024)S(1)}, f32[2048]{0:T(1024)}, u32[]{:S(2)}) copy-start(f32[2048]{0:T(1024)} %param.15) | copy-start | bytes 24580
  616.2 2.2 copy-start.11
Sparse Core Ops, SparseCore 0:
  297.7 150.0 all-reduce.5
  450.2 66.3 all-reduce.7
  546.5 67.0 all-reduce.3
